TPU v7x, 32 devices: a whole 2x2x4 slice. The times are simulated.
32 devices in a mesh: gx: 8 (over z, y), gy: 4 (over x, core).
Axes of the slice: x: 2, y: 2, z: 4, core: 2. Of those that a mesh axis runs over, the one named last changes fastest.
Arguments:
- output_one: bfloat16 [300, 12, 1024], P(None, 'gy', 'gx'), may hold values from -6 to 6
- output_two: bfloat16 [300, 12, 1024], P(None, 'gy', 'gx'), may hold values from -6 to 6
- cotan_one: bfloat16 [300, 12, 1024], P(None, 'gy', 'gx'), may hold values from -6 to 6
- cotan_two: bfloat16 [300, 12, 1024], P(None, 'gy', 'gx'), may hold values from -6 to 6
- wet_list: int32 [4, 8, 8, 48], P('gy', 'gx'), may hold values from -1 to 383, as said below
- depth_kernel: bfloat16 [300, 7, 7], replicated, may hold values from -0.875 to 0.875
- expand_weight: bfloat16 [300, 1200], replicated, may hold values from -0.375 to 0.375
- reduce_weight: bfloat16 [1200, 300], replicated, may hold values from -0.1875 to 0.1875
- level_expand: bfloat16 [4, 75, 300], replicated, may hold values from -0.75 to 0.75
- level_reduce: bfloat16 [4, 300, 75], replicated, may hold values from -0.375 to 0.375
Outputs:
- input_one: bfloat16 [300, 12, 1024], P(None, 'gy', 'gx')
- input_two: bfloat16 [300, 12, 1024], P(None, 'gy', 'gx')
- grad_input_one: bfloat16 [300, 12, 1024], P(None, 'gy', 'gx')
- grad_input_two: bfloat16 [300, 12, 1024], P(None, 'gy', 'gx')
- grad_kernel: float32 [300, 7, 7], replicated
- grad_expand: float32 [300, 1200], replicated
- grad_reduce: float32 [1200, 300], replicated
- grad_level_expand: float32 [4, 75, 300], replicated
- grad_level_reduce: float32 [4, 300, 75], replicated
Inputs may be any that keep to these rules, and one draw needn't show every extreme that they name: wet_list[j, i, p, s] is -1 or a cell index row * 128 + column inside the tile at gy index j and gx index i, listed for owner p of the same latitude row of tiles; the indices listed by one tile are distinct and are exactly its wet cells; a tile lists at most 48 cells for one owner, and one owner is listed at most 216 cells by all tiles of its row together.
All inputs are finite; a program needn't handle non-finite values.
Results may differ from a plain program's by a relative error of at most 0.0078.
Values may be sent and summed in bfloat16 or wider, within the bound.
A program may use at most 128 MiB of HBM per device.

v0:
```python
import math
import jax
import jax.numpy as jnp
from jax import lax
from jax.sharding import PartitionSpec as P

EPSILON = 1e-06


def with_halo(shard, sides, width):
    for axis, dim in sides:
        devices, length = (lax.axis_size(axis), shard.shape[dim])
        up = [(i, (i + 1) % devices) for i in range(devices)]
        down = [(j, i) for i, j in up]
        last = lax.slice_in_dim(shard, length - width, length, axis=dim)
        first = lax.slice_in_dim(shard, 0, width, axis=dim)
        before = lax.ppermute(last, axis, up)
        after = lax.ppermute(first, axis, down)
        shard = jnp.concatenate([before, shard, after], axis=dim)
    return shard


def swapped(shard, axis, stride):
    return lax.ppermute(shard, axis, [(i, i ^ 1 << stride) for i in range(lax.axis_size(axis))])


def gelu_slope(argument):
    normal_cdf = 0.5 * (1.0 + lax.erf(argument * 0.7071067811865476))
    return normal_cdf + argument * jnp.exp(-0.5 * argument * argument) * 0.3989422804014327


def level_branch(first_in, second, cot_first, cot_second, cell_mask, level_expand, level_reduce):
    groups, levels, expand_width = level_expand.shape
    column_count = first_in.shape[1]
    grouped = first_in.reshape(groups, levels, column_count)
    level_pre = jnp.einsum(
        "gls,gle->ges", grouped, level_expand, preferred_element_type=jnp.float32
    )
    active = jax.nn.gelu(level_pre, approximate=False).astype(jnp.bfloat16)
    mixed_out = jnp.einsum("ges,gel->gls", active, level_reduce, preferred_element_type=jnp.float32)
    mixed_out = mixed_out.reshape(groups * levels, column_count) * cell_mask[None, :]
    rebuilt = (second.astype(jnp.float32) - mixed_out).astype(jnp.bfloat16)
    upstream = (cot_second * cell_mask.astype(jnp.bfloat16)[None, :]).reshape(
        groups, levels, column_count
    )
    back_act = jnp.einsum(
        "gls,gel->ges", upstream, level_reduce, preferred_element_type=jnp.float32
    )
    back_pre = (back_act * gelu_slope(level_pre)).astype(jnp.bfloat16)
    back_in = jnp.einsum("ges,gle->gls", back_pre, level_expand, preferred_element_type=jnp.float32)
    total_one = (
        cot_first.astype(jnp.float32) + back_in.reshape(groups * levels, column_count)
    ).astype(jnp.bfloat16)
    grad_in = jnp.einsum("gls,ges->gle", grouped, back_pre, preferred_element_type=jnp.float32)
    grad_out = jnp.einsum("ges,gls->gel", active, upstream, preferred_element_type=jnp.float32)
    return (rebuilt, total_one, grad_in, grad_out)


def padded_rims(field_in):
    extended = with_halo(field_in, (("gx", 2), ("gy", 1)), 3)
    tile_rows = field_in.shape[1]
    at_south = lax.axis_index("gy") == 0
    at_north = lax.axis_index("gy") == lax.axis_size("gy") - 1
    row_ids = lax.broadcasted_iota(jnp.int32, (1, extended.shape[1], 1), 1)
    cut_rows = at_south & (row_ids < 3) | at_north & (row_ids >= tile_rows + 3)
    return jnp.where(cut_rows, jnp.zeros_like(extended), extended)


def mirrored(rim_rows):
    for bit_index in range(lax.axis_size("gx").bit_length() - 1):
        rim_rows = swapped(rim_rows, "gx", bit_index)
    return rim_rows


def folded_rims(field_in):
    tile_rows = field_in.shape[1]
    extended = padded_rims(field_in)
    partner = mirrored(extended[:, tile_rows : tile_rows + 3, :])
    upper_rows = partner[:, ::-1, ::-1]
    at_north = lax.axis_index("gy") == lax.axis_size("gy") - 1
    upper_rows = jnp.where(at_north, upper_rows, extended[:, tile_rows + 3 :, :])
    return jnp.concatenate([extended[:, : tile_rows + 3, :], upper_rows], axis=1)


def body(
    output_one,
    output_two,
    cotan_one,
    cotan_two,
    wet_list,
    depth_kernel,
    expand_weight,
    reduce_weight,
    level_expand,
    level_reduce,
):
    channels, tile_rows, tile_cols = output_one.shape
    tile_cells = tile_rows * tile_cols
    flat_one = output_one.reshape(channels, tile_cells)
    flat_two = output_two.reshape(channels, tile_cells)
    flat_cot_one = cotan_one.reshape(channels, tile_cells)
    flat_cot_two = cotan_two.reshape(channels, tile_cells)
    owner_count = wet_list.shape[2]
    slot_count = wet_list.shape[3]
    listing = wet_list.reshape(owner_count, slot_count)
    present = listing >= 0
    cell_index = jnp.where(present, listing, tile_cells).reshape(-1)
    wet_mask = jnp.zeros((tile_cells,), jnp.float32).at[cell_index].set(1.0, mode="drop")
    two_flat, total_flat, grad_level_in, grad_level_out = level_branch(
        flat_one, flat_two, flat_cot_one, flat_cot_two, wet_mask, level_expand, level_reduce
    )
    input_two = two_flat.reshape(channels, tile_rows, tile_cols)
    padded = folded_rims(input_two)
    wide_field = padded.astype(jnp.float32)
    kernel_wide = depth_kernel.astype(jnp.float32)
    spread = jnp.zeros((channels, tile_rows, tile_cols), jnp.float32)
    for row_tap in range(7):
        for col_tap in range(7):
            spread = (
                spread
                + kernel_wide[:, row_tap, col_tap][:, None, None]
                * wide_field[:, row_tap : row_tap + tile_rows, col_tap : col_tap + tile_cols]
            )
    spread = spread.reshape(channels, tile_cells)
    center = spread - jnp.mean(spread, axis=0, keepdims=True)
    rescale = lax.rsqrt(jnp.mean(center * center, axis=0, keepdims=True) + EPSILON)
    normal = center * rescale
    normal_half = normal.astype(jnp.bfloat16)
    contract_first = (((0,), (0,)), ((), ()))
    contract_last = (((1,), (1,)), ((), ()))
    contract_inner = (((1,), (0,)), ((), ()))
    hidden_pre = lax.dot_general(
        expand_weight, normal_half, contract_first, preferred_element_type=jnp.float32
    )
    hidden = jax.nn.gelu(hidden_pre, approximate=False).astype(jnp.bfloat16)
    update = lax.dot_general(
        reduce_weight, hidden, contract_first, preferred_element_type=jnp.float32
    )
    input_one = (flat_one.astype(jnp.float32) - update * wet_mask[None, :]).astype(jnp.bfloat16)
    upstream = total_flat * wet_mask.astype(jnp.bfloat16)[None, :]
    grad_reduce = lax.dot_general(
        hidden, upstream, contract_last, preferred_element_type=jnp.float32
    )
    back_hidden = lax.dot_general(
        reduce_weight, upstream, contract_inner, preferred_element_type=jnp.float32
    )
    back_pre = (back_hidden * gelu_slope(hidden_pre)).astype(jnp.bfloat16)
    grad_expand = lax.dot_general(
        normal_half, back_pre, contract_last, preferred_element_type=jnp.float32
    )
    back_normal = lax.dot_general(
        expand_weight, back_pre, contract_inner, preferred_element_type=jnp.float32
    )
    mean_back = jnp.mean(back_normal, axis=0, keepdims=True)
    mean_cross = jnp.mean(back_normal * normal, axis=0, keepdims=True)
    back_spread = (rescale * (back_normal - mean_back - normal * mean_cross)).astype(jnp.bfloat16)
    back_spread = back_spread.reshape(channels, tile_rows, tile_cols)
    back_field = back_spread.astype(jnp.float32)
    tap_rows = []
    for row_tap in range(7):
        tap_cols = []
        for col_tap in range(7):
            tap_cols.append(
                jnp.sum(
                    back_field
                    * wide_field[:, row_tap : row_tap + tile_rows, col_tap : col_tap + tile_cols],
                    axis=(1, 2),
                )
            )
        tap_rows.append(jnp.stack(tap_cols, axis=1))
    grad_kernel = jnp.stack(tap_rows, axis=1)
    back_padded = padded_rims(back_spread)
    back_wide = back_padded.astype(jnp.float32)
    main_part = jnp.zeros((channels, tile_rows, tile_cols), jnp.float32)
    for row_tap in range(7):
        for col_tap in range(7):
            main_part = (
                main_part
                + kernel_wide[:, row_tap, col_tap][:, None, None]
                * back_wide[
                    :, 6 - row_tap : 6 - row_tap + tile_rows, 6 - col_tap : 6 - col_tap + tile_cols
                ]
            )
    partner = mirrored(back_padded[:, tile_rows : tile_rows + 3, :])
    turned = partner[:, :, ::-1].astype(jnp.float32)
    pieces = []
    for fold_step in (3, 2, 1):
        row_total = jnp.zeros((channels, tile_cols), jnp.float32)
        for row_tap in range(3 + fold_step, min(6, 5 + fold_step) + 1):
            source_row = 5 + fold_step - row_tap
            for col_tap in range(7):
                row_total = (
                    row_total
                    + kernel_wide[:, row_tap, col_tap][:, None]
                    * turned[:, source_row, col_tap : col_tap + tile_cols]
                )
        pieces.append(row_total)
    fold_part = jnp.stack(pieces, axis=1)
    at_north = lax.axis_index("gy") == lax.axis_size("gy") - 1
    fold_part = jnp.where(at_north, fold_part, jnp.zeros_like(fold_part))
    through = main_part.at[:, tile_rows - 3 :, :].add(fold_part)
    grad_input_two = (cotan_two.astype(jnp.float32) + through).astype(jnp.bfloat16)
    summed = lax.psum(
        (grad_kernel, grad_expand, grad_reduce, grad_level_in, grad_level_out), ("gx", "gy")
    )
    factor = 1.0 / math.sqrt(tile_cells * lax.axis_size("gx") * lax.axis_size("gy"))
    return (
        input_one.reshape(channels, tile_rows, tile_cols),
        input_two,
        total_flat.reshape(channels, tile_rows, tile_cols),
        grad_input_two,
        summed[0] * factor,
        summed[1] * factor,
        summed[2] * factor,
        summed[3] * factor,
        summed[4] * factor,
    )


def solution(mesh):
    placed = (
        P(None, "gy", "gx"),
        P(None, "gy", "gx"),
        P(None, "gy", "gx"),
        P(None, "gy", "gx"),
        P("gy", "gx", None, None),
        P(),
        P(),
        P(),
        P(),
        P(),
    )
    return jax.shard_map(
        body,
        mesh=mesh,
        in_specs=placed,
        out_specs=(
            P(None, "gy", "gx"),
            P(None, "gy", "gx"),
            P(None, "gy", "gx"),
            P(None, "gy", "gx"),
            P(),
            P(),
            P(),
            P(),
            P(),
        ),
        check_vma=False,
    )
```

profile of v0, /device:TPU:0, one launch (start us, length us, event | category | flops | bytes accessed | tf_op | source)
XLA Modules:
  0.0 472.8 jit_solution(17439408598463731734)
XLA Ops:
  9.4 2.0 fusion.139
  11.4 4.2 fusion.4
  17.2 2.9 scatter_custom_fusion
  21.4 3.0 collective-permute-start
  24.4 3.0 collective-permute-start.1
  27.9 2.3 fusion.10
  33.5 4.3 collective-permute-done
  37.8 2.2 collective-permute-done.1
  40.0 1.8 pad_maximum_fusion
  50.6 2.1 copy.89
  52.9 2.1 copy.88
  55.1 4.5 maximum_select_fusion
  60.8 2.1 copy.90
  63.2 2.6 fusion.147
  65.8 6.4 %collective-permute-done.4 = bf16[300,3,134]{0,2,1:T(8,128)(2,1)S(1)} collective-permute-done((bf16[300,3,134]{0,2,1:T(8,128)(2,1)}, bf16[300,3,134]{0,2,1:T(8,128)(2,1)S(1)}, u32[]{:S(2)}, u32[]{:S(2)}) %collective-permute-start.4) | collective-permute-done | bytes 241232 | tf_op jit(solution)/shard_map/ppermute | solution.py:24
  72.2 2.7 collective-permute-start.5
  76.2 6.3 %collective-permute-done.5 = bf16[300,3,134]{0,2,1:T(8,128)(2,1)S(1)} collective-permute-done((bf16[300,3,134]{0,2,1:T(8,128)(2,1)S(1)}, bf16[300,3,134]{0,2,1:T(8,128)(2,1)S(1)}, u32[]{:S(2)}, u32[]{:S(2)}) %collective-permute-start.5) | collective-permute-done | bytes 241232 | tf_op jit(solution)/shard_map/ppermute | solution.py:24
  82.5 2.0 collective-permute-start.6
  86.4 12.0 %collective-permute-done.6 = bf16[300,3,134]{0,2,1:T(8,128)(2,1)} collective-permute-done((bf16[300,3,134]{0,2,1:T(8,128)(2,1)S(1)}, bf16[300,3,134]{0,2,1:T(8,128)(2,1)}, u32[]{:S(2)}, u32[]{:S(2)}) %collective-permute-start.6) | collective-permute-done | bytes 241232 | tf_op jit(solution)/shard_map/ppermute | solution.py:24
  98.4 2.1 copy.91
  100.6 5.4 %reverse = bf16[300,3,256]{2,1,0:T(4,128)(2,1)} reverse(bf16[300,3,256]{2,1,0:T(4,128)(2,1)} %bitcast.91), dimensions={1,2} | reverse | bytes 921600
  105.9 2.1 slice_select_fusion
  109.8 36.7 %fusion.167 = (f32[3,128]{1,0:T(4,128)S(1)}, f32[300,3,128]{2,1,0:T(4,128)S(1)}) fusion(f32[300,9,134]{2,1,0:T(8,128)S(1)} %maximum_convert_fusion, f32[300]{0:T(512)S(1)} %get-tuple-element.117, f32[300]{0:T(512)S(1)} %get-tuple-element.118, f32[300]{0:T(512)S(1)} %get-tuple-element.119, f32[300]{0:T(512)S(1)} %copy-done.35, f32[300]{0:T(512)S(1)} %copy-done.37, ...), kind=kLoop, calls=%fused_computation.387 | loop fusion | flops 11289216 | bytes 23100336 | tf_op jit(solution)/shard_map/reduce_sum | solution.py:125
  147.1 4.4 fusion.19
  154.3 31.5 %fusion.80 = (f32[300]{0:T(512)S(1)}, f32[300]{0:T(512)S(1)}, f32[300]{0:T(512)S(1)}, f32[300]{0:T(512)S(1)}, f32[300]{0:T(512)S(1)}, /*index=5*/f32[300]{0:T(51...) fusion(bf16[300,3,128]{2,1,0:T(4,128)(2,1)S(1)} %reshape.526, ...), kind=kLoop, calls=%fused_computation.165 | loop fusion | flops 3106500 | bytes 6236400 | tf_op jit(solution)/shard_map/reduce_sum | solution.py:164
  185.9 34.6 %fusion.82 = (f32[300]{0:T(512)S(1)}, f32[300]{0:T(512)S(1)}, f32[300]{0:T(512)S(1)}, f32[300]{0:T(512)S(1)}, f32[300]{0:T(512)S(1)}, /*index=5*/f32[300]{0:T(51...) fusion(bf16[300,3,128]{2,1,0:T(4,128)(2,1)S(1)} %reshape.526, ...), kind=kLoop, calls=%fused_computation.167 | loop fusion | flops 4257000 | bytes 8546400 | tf_op jit(solution)/shard_map/reduce_sum | solution.py:164
  220.4 35.5 %fusion.81 = (f32[300]{0:T(512)S(1)}, f32[300]{0:T(512)S(1)}, f32[300]{0:T(512)S(1)}, f32[300]{0:T(512)S(1)}, f32[300]{0:T(512)S(1)}, /*index=5*/f32[300]{0:T(51...) fusion(bf16[300,3,128]{2,1,0:T(4,128)(2,1)S(1)} %reshape.526, ...), kind=kLoop, calls=%fused_computation.166 | loop fusion | flops 4257000 | bytes 8546400 | tf_op jit(solution)/shard_map/reduce_sum | solution.py:164
  256.0 1.8 fusion.159
  258.7 1.7 fusion.170
  261.1 1.6 collective-permute-start.7
  262.7 3.4 collective-permute-start.8
  266.3 9.1 %collective-permute-done.7 = bf16[300,3,3]{2,1,0:T(4,128)(2,1)S(1)} collective-permute-done((bf16[300,3,3]{2,1,0:T(4,128)(2,1)}, bf16[300,3,3]{2,1,0:T(4,128)(2,1)S(1)}, u32[]{:S(2)}, u32[]{:S(2)}) %collective-permute-start.7) | collective-permute-done | bytes 5432 | tf_op jit(solution)/shard_map/ppermute | solution.py:17
  275.4 2.1 collective-permute-done.8
  279.7 6.6 %collective-permute-done.10 = bf16[300,3,134]{0,2,1:T(8,128)(2,1)S(1)} collective-permute-done((bf16[300,3,134]{0,2,1:T(8,128)(2,1)S(1)}, bf16[300,3,134]{0,2,1:T(8,128)(2,1)S(1)}, u32[]{:S(2)}, u32[]{:S(2)}) %collective-permute-start.10) | collective-permute-done | bytes 241232 | tf_op jit(solution)/shard_map/ppermute | solution.py:18
  286.7 2.4 collective-permute-done.9
  289.6 4.8 %fusion.166 = (f32[300,9,134]{2,1,0:T(8,128)}, bf16[300,9,134]{2,1,0:T(8,128)(2,1)S(1)}) fusion(bf16[300,3,134]{2,1,0:T(4,128)(2,1)S(1)} %copy.100, bf16[300,3,3]{2,1,0:T(4,128)(2,1)S(1)} %collective-permute-done.8, bf16[300,3,128]{2,1,0:T(4,128)(2,1)S(1)} %reshape.526, bf16[300,3,3]{2,1,0:T(4,128)(2,1)S(1)} %collective-permute-done.7, ...), kind=kLoop, calls=%fused_computation.386 | loop fusion | flops 4341600 | bytes 2894409 | tf_op jit(solution)/shard_map/convert_element_type | solution.py:173
  295.4 9.6 %collective-permute-done.11 = bf16[300,3,134]{0,2,1:T(8,128)(2,1)S(1)} collective-permute-done((bf16[300,3,134]{0,2,1:T(8,128)(2,1)S(1)}, bf16[300,3,134]{0,2,1:T(8,128)(2,1)S(1)}, u32[]{:S(2)}, u32[]{:S(2)}) %collective-permute-start.11) | collective-permute-done | bytes 241232 | tf_op jit(solution)/shard_map/ppermute | solution.py:24
  306.3 9.0 %collective-permute-done.12 = bf16[300,3,134]{0,2,1:T(8,128)(2,1)S(1)} collective-permute-done((bf16[300,3,134]{0,2,1:T(8,128)(2,1)S(1)}, bf16[300,3,134]{0,2,1:T(8,128)(2,1)S(1)}, u32[]{:S(2)}, u32[]{:S(2)}) %collective-permute-start.12) | collective-permute-done | bytes 241232 | tf_op jit(solution)/shard_map/ppermute | solution.py:24
  315.3 2.3 collective-permute-start.13
  317.6 41.8 %psum.35 = f32[300,7,7]{0,2,1:T(8,128)S(1)} all-reduce(f32[300,7,7]{0,2,1:T(8,128)S(1)} %constant_dynamic-update-slice_fusion), channel_id=1, replica_groups=mesh['gx'=8,'gy'=4] {'gx','gy'}, use_global_device_ids=true, to_apply=%region_54.55 | all-reduce | flops 14700 | bytes 117600 | tf_op jit(solution)/shard_map/psum | solution.py:203
  360.7 3.1 reverse.1
  364.5 14.1 %fusion.150 = f32[300,1,128]{2,1,0:T(1,128)S(1)} fusion(f32[300,3,134]{2,1,0:T(4,128)S(1)} %slice_convert_fusion, f32[300]{0:T(512)S(1)} %copy-done.65, f32[300]{0:T(512)S(1)} %copy-done.67, f32[300]{0:T(512)S(1)} %copy-done.69, f32[300]{0:T(512)S(1)} %copy-done.71, f32[300]{0:T(512)S(1)} %copy-done.59, f32[300]{0:T(512)S(1)} %copy-done.61, ...), kind=kLoop, calls=%fused_computation.300 | loop fusion | flops 1574400 | bytes 3404400 | tf_op jit(solution)/shard_map/add | solution.py:193
  378.8 9.3 %multiply_add_fusion.1 = f32[300,1,128]{2,1,0:T(1,128)S(1)} fusion(f32[300,3,134]{2,1,0:T(4,128)S(1)} %slice_convert_fusion, f32[300]{0:T(512)S(1)} %copy-done.44, f32[300]{0:T(512)S(1)} %copy-done.46, f32[300]{0:T(512)S(1)} %copy-done.48, f32[300]{0:T(512)S(1)} %copy-done.50, f32[300]{0:T(512)S(1)} %copy-done.52, f32[300]{0:T(512)S(1)} %copy-done.54, ...), kind=kLoop, calls=%fused_computation.313 | loop fusion | flops 1036800 | bytes 2320800 | tf_op jit(solution)/shard_map/add | solution.py:193
  388.1 4.6 multiply_add_fusion.2
  392.9 37.2 %fusion.86 = bf16[300,3,128]{2,1,0:T(4,128)(2,1)S(1)} fusion(f32[300,9,134]{2,1,0:T(8,128)S(1)} %bitcast.83, f32[300,1,128]{2,1,0:T(1,128)S(1)} %fusion.150, f32[300,1,128]{2,1,0:T(1,128)S(1)} %multiply_add_fusion.1, f32[300,1,128]{2,1,0:T(1,128)S(1)} %multiply_add_fusion.2, f32[300]{0:T(512)S(1)} %copy-done.30, f32[300]{0:T(512)S(1)} %copy-done.32, ...), kind=kLoop, calls=%fused_computation.172 | loop fusion | flops 11980800 | bytes 23559600 | tf_op jit(solution)/shard_map/convert_element_type | solution.py:202
  430.8 28.6 %all-reduce.3.cloned.1.call-done = (f32[300,1200]{1,0:T(8,128)}, f32[1200,300]{0,1:T(8,128)}, f32[4,75,300]{2,1,0:T(8,128)}, f32[4,300,75]{1,2,0:T(8,128)}) async-done(((f32[300,1200]{1,0:T(8,128)}, f32[1200,300]{0,1:T(8,128)}, f32[4,75,300]{2,1,0:T(8,128)}, f32[4,300,75]{1,2,0:T(8,128)}), (f32[300,1200]{1,0:T(8,128)}, f32[1200,300]{0,1:T(8,128)}, f32[4,75,300]{2,1,0:T(8,128)}, ...) | async-done | bytes 3600016 | tf_op jit(solution)/shard_map/psum | solution.py:203
  459.5 2.8 broadcast_multiply_fusion.1
  464.2 1.3 broadcast_multiply_fusion
  (379 shorter events, 37.6 us)
Async XLA Ops:
  7.2 139.9 %copy-start = (bf16[300,1200]{1,0:T(8,128)(2,1)S(1)}, bf16[300,1200]{1,0:T(8,128)(2,1)}, u32[]{:S(2)}) copy-start(bf16[300,1200]{1,0:T(8,128)(2,1)} %param.20) | copy-start | bytes 2160004
  7.2 452.3 %all-reduce.3.cloned.1.call-start = ((), (), s32[]{:S(2)}) async-start(), calls=%async_computation | async-start | bytes 8192000 | tf_op jit(solution)/shard_map/psum | solution.py:203
  16.9 10.5 %copy-start.16 = (bf16[300,3,128]{2,0,1:T(8,128)(2,1)S(1)}, bf16[300,3,128]{2,0,1:T(8,128)(2,1)}, u32[]{:S(2)}) copy-start(bf16[300,3,128]{2,0,1:T(8,128)(2,1)} %param.17) | copy-start | bytes 691204
  17.1 10.6 %copy-start.18 = (bf16[300,3,128]{2,0,1:T(8,128)(2,1)S(1)}, bf16[300,3,128]{2,0,1:T(8,128)(2,1)}, u32[]{:S(2)}) copy-start(bf16[300,3,128]{2,0,1:T(8,128)(2,1)} %param.16) | copy-start | bytes 691204
  21.4 16.4 %collective-permute-start = (bf16[300,3,3]{2,1,0:T(4,128)(2,1)}, bf16[300,3,3]{2,1,0:T(4,128)(2,1)S(1)}, u32[]{:S(2)}, u32[]{:S(2)}) collective-permute-start(bf16[300,3,3]{2,1,0:T(4,128)(2,1)} %get-tuple-element.175), channel_id=1, source_target_pairs={{0,4},{4,8},{8,12},{12,16},{16,20},{20,24},{24,28},{28,0},{1,5},{5... | collective-permute-start | bytes 16208 | tf_op jit(solution)/shard_map/ppermute | solution.py:17
  24.4 15.6 %collective-permute-start.1 = (bf16[300,3,3]{2,1,0:T(4,128)(2,1)}, bf16[300,3,3]{2,1,0:T(4,128)(2,1)}, u32[]{:S(2)}, u32[]{:S(2)}) collective-permute-start(bf16[300,3,3]{2,1,0:T(4,128)(2,1)} %get-tuple-element.176), channel_id=1, source_target_pairs={{4,0},{8,4},{12,8},{16,12},{20,16},{24,20},{28,24},{0,28},{5,1},{9... | collective-permute-start | bytes 16208 | tf_op jit(solution)/shard_map/ppermute | solution.py:18
  42.9 7.8 %collective-permute-start.3 = (bf16[300,3,134]{0,2,1:T(8,128)(2,1)}, bf16[300,3,134]{0,2,1:T(8,128)(2,1)}, u32[]{:S(2)}, u32[]{:S(2)}) collective-permute-start(bf16[300,3,134]{0,2,1:T(8,128)(2,1)} %copy.86), channel_id=1, source_target_pairs={{1,0},{2,1},{3,2},{0,3},{5,4},{6,5},{7,6},{4,7},{9,8},{10,9},{11,1... | collective-permute-start | bytes 723608 | tf_op jit(solution)/shard_map/ppermute | solution.py:18
  42.9 10.1 %collective-permute-start.2 = (bf16[300,3,134]{0,2,1:T(8,128)(2,1)}, bf16[300,3,134]{0,2,1:T(8,128)(2,1)}, u32[]{:S(2)}, u32[]{:S(2)}) collective-permute-start(bf16[300,3,134]{0,2,1:T(8,128)(2,1)} %copy.86), channel_id=1, source_target_pairs={{0,1},{1,2},{2,3},{3,0},{4,5},{5,6},{6,7},{7,4},{8,9},{9,10},{10,1... | collective-permute-start | bytes 723608 | tf_op jit(solution)/shard_map/ppermute | solution.py:17
  50.6 58.8 %copy-start.29 = (f32[300]{0:T(512)}, f32[300]{0:T(512)S(1)}, u32[]{:S(2)}) copy-start(f32[300]{0:T(512)S(1)} %get-tuple-element.117) | copy-start | bytes 3604
  50.6 58.8 %copy-start.31 = (f32[300]{0:T(512)}, f32[300]{0:T(512)S(1)}, u32[]{:S(2)}) copy-start(f32[300]{0:T(512)S(1)} %get-tuple-element.118) | copy-start | bytes 3604
  50.6 58.8 %copy-start.33 = (f32[300]{0:T(512)}, f32[300]{0:T(512)S(1)}, u32[]{:S(2)}) copy-start(f32[300]{0:T(512)S(1)} %get-tuple-element.119) | copy-start | bytes 3604
  59.6 15.3 %copy-start.14 = (bf16[4,75,384]{2,1,0:T(8,128)(2,1)S(1)}, bf16[4,75,384]{2,1,0:T(8,128)(2,1)}, u32[]{:S(2)}) copy-start(bf16[4,75,384]{2,1,0:T(8,128)(2,1)} %copy-done.13) | copy-start | bytes 691204
  62.9 12.1 %copy-start.6 = (bf16[4,300,384]{2,1,0:T(8,128)(2,1)S(1)}, bf16[4,300,384]{2,1,0:T(8,128)(2,1)}, u32[]{:S(2)}) copy-start(bf16[4,300,384]{2,1,0:T(8,128)(2,1)} %copy-done.5) | copy-start | bytes 2764804
  62.9 21.7 %copy-start.8 = (f32[300,384]{1,0:T(8,128)S(1)}, f32[300,384]{1,0:T(8,128)}, u32[]{:S(2)}) copy-start(f32[300,384]{1,0:T(8,128)} %reshape.525) | copy-start | bytes 1382404
  62.9 21.7 %copy-start.9 = (f32[38,8,3,128]{3,1,2,0:T(8,128)S(1)}, f32[38,8,3,128]{3,1,2,0:T(8,128)}, u32[]{:S(2)}) copy-start(f32[38,8,3,128]{3,1,2,0:T(8,128)} %copy.111) | copy-start | bytes 1400836
  62.9 9.4 %collective-permute-start.4 = (bf16[300,3,134]{0,2,1:T(8,128)(2,1)}, bf16[300,3,134]{0,2,1:T(8,128)(2,1)S(1)}, u32[]{:S(2)}, u32[]{:S(2)}) collective-permute-start(bf16[300,3,134]{0,2,1:T(8,128)(2,1)} %copy.90), channel_id=1, source_target_pairs={{0,4},{4,0},{8,12},{12,8},{16,20},{20,16},{24,28},{28,24},{1,5},{5... | collective-permute-start | bytes 723608 | tf_op jit(solution)/shard_map/ppermute | solution.py:24
  72.2 10.3 %collective-permute-start.5 = (bf16[300,3,134]{0,2,1:T(8,128)(2,1)S(1)}, bf16[300,3,134]{0,2,1:T(8,128)(2,1)S(1)}, u32[]{:S(2)}, u32[]{:S(2)}) collective-permute-start(bf16[300,3,134]{0,2,1:T(8,128)(2,1)S(1)} %collective-permute-done.4), channel_id=1, source_target_pairs={{0,8},{4,12},{8,0},{12,4},{16,24},{20,28},{24,16},{28,20},{1,9},{5... | collective-permute-start | bytes 723608 | tf_op jit(solution)/shard_map/ppermute | solution.py:24
  82.5 15.9 %collective-permute-start.6 = (bf16[300,3,134]{0,2,1:T(8,128)(2,1)S(1)}, bf16[300,3,134]{0,2,1:T(8,128)(2,1)}, u32[]{:S(2)}, u32[]{:S(2)}) collective-permute-start(bf16[300,3,134]{0,2,1:T(8,128)(2,1)S(1)} %collective-permute-done.5), channel_id=1, source_target_pairs={{0,16},{4,20},{8,24},{12,28},{16,0},{20,4},{24,8},{28,12},{1,17},{... | collective-permute-start | bytes 723608 | tf_op jit(solution)/shard_map/ppermute | solution.py:24
  109.4 37.2 %copy-start.2 = (f32[300,9,134]{2,1,0:T(8,128)}, f32[300,9,134]{2,1,0:T(8,128)S(1)}, u32[]{:S(2)}) copy-start(f32[300,9,134]{2,1,0:T(8,128)S(1)} %maximum_convert_fusion) | copy-start | bytes 4341604
  220.4 35.5 %copy-start.75 = (f32[384]{0:T(512)S(1)}, f32[384]{0:T(512)}, u32[]{:S(2)}) copy-start(f32[384]{0:T(512)} %copy-done.74) | copy-start | bytes 4612
  220.4 35.5 %copy-start.77 = (f32[384]{0:T(512)S(1)}, f32[384]{0:T(512)}, u32[]{:S(2)}) copy-start(f32[384]{0:T(512)} %copy-done.76) | copy-start | bytes 4612
  261.1 14.3 %collective-permute-start.7 = (bf16[300,3,3]{2,1,0:T(4,128)(2,1)}, bf16[300,3,3]{2,1,0:T(4,128)(2,1)S(1)}, u32[]{:S(2)}, u32[]{:S(2)}) collective-permute-start(bf16[300,3,3]{2,1,0:T(4,128)(2,1)} %get-tuple-element.173), channel_id=1, source_target_pairs={{0,4},{4,8},{8,12},{12,16},{16,20},{20,24},{24,28},{28,0},{1,5},{5... | collective-permute-start | bytes 16208 | tf_op jit(solution)/shard_map/ppermute | solution.py:17
  262.7 14.8 %collective-permute-start.8 = (bf16[300,3,3]{2,1,0:T(4,128)(2,1)S(1)}, bf16[300,3,3]{2,1,0:T(4,128)(2,1)S(1)}, u32[]{:S(2)}, u32[]{:S(2)}) collective-permute-start(bf16[300,3,3]{2,1,0:T(4,128)(2,1)S(1)} %get-tuple-element.174), channel_id=1, source_target_pairs={{4,0},{8,4},{12,8},{16,12},{20,16},{24,20},{28,24},{0,28},{5,1},{9... | collective-permute-start | bytes 16208 | tf_op jit(solution)/shard_map/ppermute | solution.py:18
  266.3 23.3 %copy-start.116 = (pred[9]{0:T(512)(128)(4,1)S(1)}, pred[9]{0:T(512)(128)(4,1)}, u32[]{:S(2)}) copy-start(pred[9]{0:T(512)(128)(4,1)} %and_or_fusion) | copy-start | bytes 31
  278.8 7.6 %collective-permute-start.10 = (bf16[300,3,134]{0,2,1:T(8,128)(2,1)S(1)}, bf16[300,3,134]{0,2,1:T(8,128)(2,1)S(1)}, u32[]{:S(2)}, u32[]{:S(2)}) collective-permute-start(bf16[300,3,134]{0,2,1:T(8,128)(2,1)S(1)} %copy.97), channel_id=1, source_target_pairs={{1,0},{2,1},{3,2},{0,3},{5,4},{6,5},{7,6},{4,7},{9,8},{10,9},{11,1... | collective-permute-start | bytes 723608 | tf_op jit(solution)/shard_map/ppermute | solution.py:18
  279.5 9.7 %collective-permute-start.9 = (bf16[300,3,134]{0,2,1:T(8,128)(2,1)S(1)}, bf16[300,3,134]{0,2,1:T(8,128)(2,1)S(1)}, u32[]{:S(2)}, u32[]{:S(2)}) collective-permute-start(bf16[300,3,134]{0,2,1:T(8,128)(2,1)S(1)} %copy.97), channel_id=1, source_target_pairs={{0,1},{1,2},{2,3},{3,0},{4,5},{5,6},{6,7},{7,4},{8,9},{9,10},{10,1... | collective-permute-start | bytes 723608 | tf_op jit(solution)/shard_map/ppermute | solution.py:17
  295.1 9.9 %collective-permute-start.11 = (bf16[300,3,134]{0,2,1:T(8,128)(2,1)S(1)}, bf16[300,3,134]{0,2,1:T(8,128)(2,1)S(1)}, u32[]{:S(2)}, u32[]{:S(2)}) collective-permute-start(bf16[300,3,134]{0,2,1:T(8,128)(2,1)S(1)} %copy.101), channel_id=1, source_target_pairs={{0,4},{4,0},{8,12},{12,8},{16,20},{20,16},{24,28},{28,24},{1,5},{5... | collective-permute-start | bytes 723608 | tf_op jit(solution)/shard_map/ppermute | solution.py:24
  305.0 10.3 %collective-permute-start.12 = (bf16[300,3,134]{0,2,1:T(8,128)(2,1)S(1)}, bf16[300,3,134]{0,2,1:T(8,128)(2,1)S(1)}, u32[]{:S(2)}, u32[]{:S(2)}) collective-permute-start(bf16[300,3,134]{0,2,1:T(8,128)(2,1)S(1)} %collective-permute-done.11), channel_id=1, source_target_pairs={{0,8},{4,12},{8,0},{12,4},{16,24},{20,28},{24,16},{28,20},{1,9},{5... | collective-permute-start | bytes 723608 | tf_op jit(solution)/shard_map/ppermute | solution.py:24
  306.2 86.5 %slice-start = ((s8[4915200]{0:T(1024)(128)(4,1)}), s8[720896]{0:T(1024)(128)(4,1)S(1)}, s32[]{:S(2)}) async-start(s8[4915200]{0:T(1024)(128)(4,1)} %bitcast.82), calls=%async_computation.1 | async-start | bytes 1441792
  315.3 45.0 %collective-permute-start.13 = (bf16[300,3,134]{0,2,1:T(8,128)(2,1)S(1)}, bf16[300,3,134]{0,2,1:T(8,128)(2,1)S(1)}, u32[]{:S(2)}, u32[]{:S(2)}) collective-permute-start(bf16[300,3,134]{0,2,1:T(8,128)(2,1)S(1)} %collective-permute-done.12), channel_id=1, source_target_pairs={{0,16},{4,20},{8,24},{12,28},{16,0},{20,4},{24,8},{28,12},{1,17},{... | collective-permute-start | bytes 723608 | tf_op jit(solution)/shard_map/ppermute | solution.py:24
  363.8 28.9 %slice-start.1 = ((s8[4915200]{0:T(1024)(128)(4,1)}), s8[4194304]{0:T(1024)(128)(4,1)S(1)}, s32[]{:S(2)}) async-start(s8[4915200]{0:T(1024)(128)(4,1)} %bitcast.82), calls=%async_computation.2 | async-start | bytes 8388608
  378.6 14.1 %copy-start.17 = (bf16[300,3,128]{2,0,1:T(8,128)(2,1)S(1)}, bf16[300,3,128]{2,0,1:T(8,128)(2,1)}, u32[]{:S(2)}) copy-start(bf16[300,3,128]{2,0,1:T(8,128)(2,1)} %param.17) | copy-start | bytes 691204
  378.6 14.1 %copy-start.79 = (f32[300]{0:T(512)S(1)}, f32[300]{0:T(512)}, u32[]{:S(2)}) copy-start(f32[300]{0:T(512)} %get-tuple-element.154) | copy-start | bytes 3604
  378.6 14.1 %copy-start.81 = (f32[300]{0:T(512)S(1)}, f32[300]{0:T(512)}, u32[]{:S(2)}) copy-start(f32[300]{0:T(512)} %get-tuple-element.155) | copy-start | bytes 3604
  378.6 14.1 %copy-start.83 = (f32[300]{0:T(512)S(1)}, f32[300]{0:T(512)}, u32[]{:S(2)}) copy-start(f32[300]{0:T(512)} %get-tuple-element.156) | copy-start | bytes 3604
  378.7 14.1 %copy-start.85 = (f32[300]{0:T(512)S(1)}, f32[300]{0:T(512)}, u32[]{:S(2)}) copy-start(f32[300]{0:T(512)} %get-tuple-element.157) | copy-start | bytes 3604
  378.7 14.1 %copy-start.87 = (f32[300]{0:T(512)S(1)}, f32[300]{0:T(512)}, u32[]{:S(2)}) copy-start(f32[300]{0:T(512)} %get-tuple-element.158) | copy-start | bytes 3604
  378.7 14.1 %copy-start.89 = (f32[300]{0:T(512)S(1)}, f32[300]{0:T(512)}, u32[]{:S(2)}) copy-start(f32[300]{0:T(512)} %get-tuple-element.159) | copy-start | bytes 3604
  378.7 14.1 %copy-start.91 = (f32[300]{0:T(512)S(1)}, f32[300]{0:T(512)}, u32[]{:S(2)}) copy-start(f32[300]{0:T(512)} %get-tuple-element.160) | copy-start | bytes 3604
  378.7 14.1 %copy-start.93 = (f32[300]{0:T(512)S(1)}, f32[300]{0:T(512)}, u32[]{:S(2)}) copy-start(f32[300]{0:T(512)} %get-tuple-element.161) | copy-start | bytes 3604
  378.7 14.1 %copy-start.95 = (f32[300]{0:T(512)S(1)}, f32[300]{0:T(512)}, u32[]{:S(2)}) copy-start(f32[300]{0:T(512)} %get-tuple-element.162) | copy-start | bytes 3604
  378.7 14.1 %copy-start.97 = (f32[300]{0:T(512)S(1)}, f32[300]{0:T(512)}, u32[]{:S(2)}) copy-start(f32[300]{0:T(512)} %get-tuple-element.163) | copy-start | bytes 3604
  378.7 14.1 %copy-start.99 = (f32[300]{0:T(512)S(1)}, f32[300]{0:T(512)}, u32[]{:S(2)}) copy-start(f32[300]{0:T(512)} %get-tuple-element.164) | copy-start | bytes 3604
  378.7 14.1 %copy-start.101 = (f32[300]{0:T(512)S(1)}, f32[300]{0:T(512)}, u32[]{:S(2)}) copy-start(f32[300]{0:T(512)} %get-tuple-element.135) | copy-start | bytes 3604
  378.7 14.1 %copy-start.103 = (f32[300]{0:T(512)S(1)}, f32[300]{0:T(512)}, u32[]{:S(2)}) copy-start(f32[300]{0:T(512)} %get-tuple-element.139) | copy-start | bytes 3604
  378.8 14.1 %copy-start.105 = (f32[300]{0:T(512)S(1)}, f32[300]{0:T(512)}, u32[]{:S(2)}) copy-start(f32[300]{0:T(512)} %get-tuple-element.140) | copy-start | bytes 3604
  378.8 14.1 %copy-start.107 = (f32[300]{0:T(512)S(1)}, f32[300]{0:T(512)}, u32[]{:S(2)}) copy-start(f32[300]{0:T(512)} %get-tuple-element.141) | copy-start | bytes 3604
  378.8 14.1 %copy-start.109 = (f32[300]{0:T(512)S(1)}, f32[300]{0:T(512)}, u32[]{:S(2)}) copy-start(f32[300]{0:T(512)} %get-tuple-element.142) | copy-start | bytes 3604
  (86 other events, 250.1 us)
Sparse Core Ops, SparseCore 0:
  306.4 153.0 all-reduce.2
where the time goes:
time: 480 us; the launch traced here: 473 us
  other arithmetic  232 us (48%)
  waiting for transfers between devices  98.9 us (21%)
  local copies, waits for them, and re-layouts  44 us (9%)
  blocking collectives  41.8 us (9%)
  starting transfers between devices  20.4 us (4%)
  matrix products  19.1 us (4%)
  between operations  16.9 us (4%)
    reduce_sum x3, other arithmetic, body(): jnp.sum(back_field * wide_field[:, row_tap:row_tap + tile_rows, col_tap:c...  102 us
    ppermute x6, waiting for transfers between devices, swapped(): lax.ppermute(shard, axis, [(i, i ^ 1 << stride) for i in range(lax.axis_s...  43.3 us
    psum x1, blocking collectives, body(): lax.psum((grad_kernel, grad_expand, grad_reduce, grad_level_in, grad_leve...  41.8 us
    convert_element_type x1, other arithmetic, body(): (cotan_two.astype(jnp.float32) + through).astype(jnp.bfloat16)  37.2 us
    reduce_sum x1, other arithmetic, body(): center = spread - jnp.mean(spread, axis=0, keepdims=True)  36.7 us
    psum x1, waiting for transfers between devices, body(): lax.psum((grad_kernel, grad_expand, grad_reduce, grad_level_in, grad_leve...  28.6 us
    add x3, other arithmetic, body(): row_total + kernel_wide[:, row_tap, col_tap][:, None] * turned[:, source_...  28 us
    unnamed x260, local copies, waits for them, and re-layouts  18.8 us
  transfers between devices with their start and end apart: 15, of which 13 were waited for; matrix products, arithmetic and copies ran while one was open for 19% of the time, Pallas kernels for 0%

commit v1 on v0

--- a/solution.py
+++ b/solution.py
@@ -201,7 +201,7 @@
     through = main_part.at[:, tile_rows - 3 :, :].add(fold_part)
     grad_input_two = (cotan_two.astype(jnp.float32) + through).astype(jnp.bfloat16)
     summed = lax.psum(
-        (grad_kernel, grad_expand, grad_reduce, grad_level_in, grad_level_out), ("gx", "gy")
+        lax.psum((grad_kernel, grad_expand, grad_reduce, grad_level_in, grad_level_out), "gy"), "gx"
     )
     factor = 1.0 / math.sqrt(tile_cells * lax.axis_size("gx") * lax.axis_size("gy"))
     return (

time: 480 us -> 547 us (1.14)
  other arithmetic: 232 us -> 266 us
  waiting for transfers between devices: 98.9 us -> 119 us
  blocking collectives: 41.8 us -> 53.1 us
    psum x0 -> x1, waiting for transfers between devices: none -> 53.9 us  [body(): lax.psum(lax.psum((grad_kernel, grad_expand, grad_reduce, grad_level_in,...]
    psum x0 -> x1, blocking collectives: none -> 38.8 us  [body(): lax.psum(lax.psum((grad_kernel, grad_expand, grad_reduce, grad_level_in,...]
    convert_element_type x1, other arithmetic: 37.2 us -> 70.2 us  [body(): (cotan_two.astype(jnp.float32) + through).astype(jnp.bfloat16)]
    psum x1, waiting for transfers between devices: 28.6 us -> 0.02 us  [body(): lax.psum((grad_kernel, grad_expand, grad_reduce, grad_level_in, grad_leve...]
    psum x1, blocking collectives: 41.8 us -> 14.3 us  [body(): lax.psum((grad_kernel, grad_expand, grad_reduce, grad_level_in, grad_leve...]
    ppermute x6, waiting for transfers between devices: 43.3 us -> 32.8 us  [swapped(): lax.ppermute(shard, axis, [(i, i ^ 1 << stride) for i in range(lax.axis_s...]
    ppermute x4, waiting for transfers between devices: 10.9 us -> 18.6 us  [with_halo(): after = lax.ppermute(first, axis, down)]
    unnamed x260 -> x280, local copies, waits for them, and re-layouts: 18.8 us -> 19.5 us
  transfers between devices with their start and end apart: 15 -> 16, of which waited for: 13 -> 12; matrix products, arithmetic and copies ran while one was open for 19% -> 25% of each run, Pallas kernels for 0% -> 0%
where the time goes in v1:
time: 547 us; the launch traced here: 540 us
  other arithmetic  266 us (49%)
  waiting for transfers between devices  119 us (22%)
  blocking collectives  53.1 us (10%)
  local copies, waits for them, and re-layouts  44.9 us (8%)
  starting transfers between devices  21 us (4%)
  matrix products  19.1 us (3%)
  between operations  17 us (3%)
    reduce_sum x3, other arithmetic, body(): jnp.sum(back_field * wide_field[:, row_tap:row_tap + tile_rows, col_tap:c...  102 us
    convert_element_type x1, other arithmetic, body(): (cotan_two.astype(jnp.float32) + through).astype(jnp.bfloat16)  70.2 us
    psum x1, waiting for transfers between devices, body(): lax.psum(lax.psum((grad_kernel, grad_expand, grad_reduce, grad_level_in,...  53.9 us
    psum x1, blocking collectives, body(): lax.psum(lax.psum((grad_kernel, grad_expand, grad_reduce, grad_level_in,...  38.8 us
    reduce_sum x1, other arithmetic, body(): center = spread - jnp.mean(spread, axis=0, keepdims=True)  36.7 us
    ppermute x6, waiting for transfers between devices, swapped(): lax.ppermute(shard, axis, [(i, i ^ 1 << stride) for i in range(lax.axis_s...  32.8 us
    add x3, other arithmetic, body(): row_total + kernel_wide[:, row_tap, col_tap][:, None] * turned[:, source_...  28 us
    unnamed x280, local copies, waits for them, and re-layouts  19.5 us
  transfers between devices with their start and end apart: 16, of which 12 were waited for; matrix products, arithmetic and copies ran while one was open for 25% of the time, Pallas kernels for 0%

profile of v1, /device:TPU:0, one launch (start us, length us, event | category | flops | bytes accessed | tf_op | source)
XLA Modules:
  0.0 540.2 jit_solution(7123540591526650969)
XLA Ops:
  9.4 2.0 fusion.139
  11.4 4.2 fusion.4
  17.2 2.9 scatter_custom_fusion
  21.4 3.0 collective-permute-start
  24.4 3.0 collective-permute-start.1
  27.9 2.3 fusion.10
  33.4 4.4 collective-permute-done
  37.8 2.2 collective-permute-done.1
  40.0 1.8 pad_maximum_fusion
  50.7 2.1 copy.89
  52.9 2.1 copy.88
  55.1 4.5 maximum_select_fusion
  60.8 2.1 copy.90
  63.2 2.6 fusion.147
  65.8 6.4 %collective-permute-done.4 = bf16[300,3,134]{0,2,1:T(8,128)(2,1)S(1)} collective-permute-done((bf16[300,3,134]{0,2,1:T(8,128)(2,1)}, bf16[300,3,134]{0,2,1:T(8,128)(2,1)S(1)}, u32[]{:S(2)}, u32[]{:S(2)}) %collective-permute-start.4) | collective-permute-done | bytes 241232 | tf_op jit(solution)/shard_map/ppermute | solution.py:24
  72.2 2.7 collective-permute-start.5
  76.2 6.3 %collective-permute-done.5 = bf16[300,3,134]{0,2,1:T(8,128)(2,1)S(1)} collective-permute-done((bf16[300,3,134]{0,2,1:T(8,128)(2,1)S(1)}, bf16[300,3,134]{0,2,1:T(8,128)(2,1)S(1)}, u32[]{:S(2)}, u32[]{:S(2)}) %collective-permute-start.5) | collective-permute-done | bytes 241232 | tf_op jit(solution)/shard_map/ppermute | solution.py:24
  82.5 2.0 collective-permute-start.6
  86.4 12.0 %collective-permute-done.6 = bf16[300,3,134]{0,2,1:T(8,128)(2,1)} collective-permute-done((bf16[300,3,134]{0,2,1:T(8,128)(2,1)S(1)}, bf16[300,3,134]{0,2,1:T(8,128)(2,1)}, u32[]{:S(2)}, u32[]{:S(2)}) %collective-permute-start.6) | collective-permute-done | bytes 241232 | tf_op jit(solution)/shard_map/ppermute | solution.py:24
  98.4 2.1 copy.91
  100.6 5.4 reverse
  105.9 2.1 slice_select_fusion
  109.8 36.7 %fusion.167 = (f32[3,128]{1,0:T(4,128)S(1)}, f32[300,3,128]{2,1,0:T(4,128)S(1)}) fusion(f32[300,9,134]{2,1,0:T(8,128)S(1)} %maximum_convert_fusion, f32[300]{0:T(512)S(1)} %get-tuple-element.117, f32[300]{0:T(512)S(1)} %get-tuple-element.118, f32[300]{0:T(512)S(1)} %get-tuple-element.119, f32[300]{0:T(512)S(1)} %copy-done.35, f32[300]{0:T(512)S(1)} %copy-done.37, ...), kind=kLoop, calls=%fused_computation.387 | loop fusion | flops 11289216 | bytes 23100336 | tf_op jit(solution)/shard_map/reduce_sum | solution.py:125
  147.1 4.4 fusion.19
  154.3 31.5 %fusion.80 = (f32[300]{0:T(512)S(1)}, f32[300]{0:T(512)S(1)}, f32[300]{0:T(512)S(1)}, f32[300]{0:T(512)S(1)}, f32[300]{0:T(512)S(1)}, /*index=5*/f32[300]{0:T(51...) fusion(bf16[300,3,128]{2,1,0:T(4,128)(2,1)S(1)} %reshape.526, ...), kind=kLoop, calls=%fused_computation.165 | loop fusion | flops 3106500 | bytes 6236400 | tf_op jit(solution)/shard_map/reduce_sum | solution.py:164
  185.9 34.6 %fusion.82 = (f32[300]{0:T(512)S(1)}, f32[300]{0:T(512)S(1)}, f32[300]{0:T(512)S(1)}, f32[300]{0:T(512)S(1)}, f32[300]{0:T(512)S(1)}, /*index=5*/f32[300]{0:T(51...) fusion(bf16[300,3,128]{2,1,0:T(4,128)(2,1)S(1)} %reshape.526, ...), kind=kLoop, calls=%fused_computation.167 | loop fusion | flops 4257000 | bytes 8546400 | tf_op jit(solution)/shard_map/reduce_sum | solution.py:164
  220.4 36.0 %fusion.81 = (f32[300]{0:T(512)}, f32[300]{0:T(512)S(1)}, f32[300]{0:T(512)S(1)}, f32[300]{0:T(512)S(1)}, f32[300]{0:T(512)S(1)}, /*index=5*/f32[300]{0:T(512)S(...) fusion(bf16[300,3,128]{2,1,0:T(4,128)(2,1)S(1)} %reshape.526, ...), kind=kLoop, calls=%fused_computation.166 | loop fusion | flops 4257000 | bytes 8546400 | tf_op jit(solution)/shard_map/reduce_sum | solution.py:164
  256.5 1.7 fusion.159
  258.5 1.7 fusion.170
  260.6 1.6 collective-permute-start.7
  262.2 3.2 collective-permute-start.8
  265.9 8.6 %collective-permute-done.7 = bf16[300,3,3]{2,1,0:T(4,128)(2,1)S(1)} collective-permute-done((bf16[300,3,3]{2,1,0:T(4,128)(2,1)S(1)}, bf16[300,3,3]{2,1,0:T(4,128)(2,1)S(1)}, u32[]{:S(2)}, u32[]{:S(2)}) %collective-permute-start.7) | collective-permute-done | bytes 5432 | tf_op jit(solution)/shard_map/ppermute | solution.py:17
  274.6 2.2 collective-permute-done.8
  279.2 14.2 %collective-permute-done.10 = bf16[300,3,134]{0,2,1:T(8,128)(2,1)} collective-permute-done((bf16[300,3,134]{0,2,1:T(8,128)(2,1)S(1)}, bf16[300,3,134]{0,2,1:T(8,128)(2,1)}, u32[]{:S(2)}, u32[]{:S(2)}) %collective-permute-start.10) | collective-permute-done | bytes 241232 | tf_op jit(solution)/shard_map/ppermute | solution.py:18
  293.3 1.3 copy.100
  295.8 5.4 %fusion.166 = (f32[300,9,134]{2,1,0:T(8,128)}, bf16[300,9,134]{2,1,0:T(8,128)(2,1)S(1)}) fusion(bf16[300,3,134]{2,1,0:T(4,128)(2,1)S(1)} %copy.100, bf16[300,3,3]{2,1,0:T(4,128)(2,1)S(1)} %collective-permute-done.8, bf16[300,3,128]{2,1,0:T(4,128)(2,1)S(1)} %reshape.526, bf16[300,3,3]{2,1,0:T(4,128)(2,1)S(1)} %collective-permute-done.7, ...), kind=kLoop, calls=%fused_computation.386 | loop fusion | flops 4341600 | bytes 2894409 | tf_op jit(solution)/shard_map/convert_element_type | solution.py:173
  302.0 14.3 %psum.70 = f32[300,7,7]{0,2,1:T(8,128)S(1)} all-reduce(f32[300,7,7]{0,2,1:T(8,128)S(1)} %constant_dynamic-update-slice_fusion), channel_id=1, replica_groups=mesh['gx'=8,'gy'=4] {'gy'}, use_global_device_ids=true, to_apply=%region_54.55 | all-reduce | flops 14700 | bytes 117600 | tf_op jit(solution)/shard_map/psum | solution.py:204
  318.0 8.0 %collective-permute-done.12 = bf16[300,3,134]{0,2,1:T(8,128)(2,1)S(1)} collective-permute-done((bf16[300,3,134]{0,2,1:T(8,128)(2,1)}, bf16[300,3,134]{0,2,1:T(8,128)(2,1)S(1)}, u32[]{:S(2)}, u32[]{:S(2)}) %collective-permute-start.12) | collective-permute-done | bytes 241232 | tf_op jit(solution)/shard_map/ppermute | solution.py:24
  326.0 2.1 collective-permute-start.13
  328.1 38.8 %psum.71 = f32[300,7,7]{0,2,1:T(8,128)S(1)} all-reduce(f32[300,7,7]{0,2,1:T(8,128)S(1)} %psum.70), channel_id=1, replica_groups=mesh['gx'=8,'gy'=4] {'gx'}, use_global_device_ids=true, to_apply=%region_55.56 | all-reduce | flops 14700 | bytes 117600 | tf_op jit(solution)/shard_map/psum | solution.py:203
  368.8 3.1 reverse.1
  373.2 9.3 %multiply_add_fusion.1 = f32[300,1,128]{2,1,0:T(1,128)S(1)} fusion(f32[300,3,134]{2,1,0:T(4,128)S(1)} %slice_convert_fusion, f32[300]{0:T(512)S(1)} %copy-done.44, f32[300]{0:T(512)S(1)} %copy-done.46, f32[300]{0:T(512)S(1)} %copy-done.48, f32[300]{0:T(512)S(1)} %copy-done.50, f32[300]{0:T(512)S(1)} %copy-done.52, f32[300]{0:T(512)S(1)} %copy-done.54, ...), kind=kLoop, calls=%fused_computation.313 | loop fusion | flops 1036800 | bytes 2320800 | tf_op jit(solution)/shard_map/add | solution.py:193
  382.6 4.6 multiply_add_fusion.2
  387.5 14.1 %fusion.150 = f32[300,1,128]{2,1,0:T(1,128)S(1)} fusion(f32[300,3,134]{2,1,0:T(4,128)S(1)} %slice_convert_fusion, f32[300]{0:T(512)S(1)} %copy-done.65, f32[300]{0:T(512)S(1)} %copy-done.67, f32[300]{0:T(512)S(1)} %copy-done.69, f32[300]{0:T(512)S(1)} %copy-done.71, f32[300]{0:T(512)S(1)} %copy-done.59, f32[300]{0:T(512)S(1)} %copy-done.61, ...), kind=kLoop, calls=%fused_computation.300 | loop fusion | flops 1574400 | bytes 3404400 | tf_op jit(solution)/shard_map/add | solution.py:193
  402.0 70.2 %fusion.86 = bf16[300,3,128]{2,1,0:T(4,128)(2,1)S(1)} fusion(f32[300,9,134]{2,1,0:T(8,128)} %get-tuple-element.173, f32[300,1,128]{2,1,0:T(1,128)S(1)} %fusion.150, f32[300,1,128]{2,1,0:T(1,128)S(1)} %multiply_add_fusion.1, f32[300,1,128]{2,1,0:T(1,128)S(1)} %multiply_add_fusion.2, f32[300]{0:T(512)S(1)} %copy-done.30, f32[300]{0:T(512)S(1)} %copy-done.32, ...), kind=kLoop, calls=%fused_computation.172 | loop fusion | flops 11980800 | bytes 23559600 | tf_op jit(solution)/shard_map/convert_element_type | solution.py:202
  472.9 53.9 %all-reduce.5.cloned.1.call-done = (f32[300,1200]{1,0:T(8,128)}, f32[1200,300]{0,1:T(8,128)}, f32[4,75,300]{2,1,0:T(8,128)}, f32[4,300,75]{1,2,0:T(8,128)}) async-done(((f32[300,1200]{1,0:T(8,128)}, f32[1200,300]{0,1:T(8,128)}, f32[4,75,300]{2,1,0:T(8,128)}, f32[4,300,75]{1,2,0:T(8,128)}), (f32[300,1200]{1,0:T(8,128)}, f32[1200,300]{0,1:T(8,128)}, f32[4,75,300]{2,1,0:T(8,128)}, ...) | async-done | bytes 3600016 | tf_op jit(solution)/shard_map/psum | solution.py:203
  526.8 2.8 broadcast_multiply_fusion.1
  531.5 1.3 broadcast_multiply_fusion
  (402 shorter events, 39.0 us)
Async XLA Ops:
  7.2 139.9 %copy-start = (bf16[300,1200]{1,0:T(8,128)(2,1)S(1)}, bf16[300,1200]{1,0:T(8,128)(2,1)}, u32[]{:S(2)}) copy-start(bf16[300,1200]{1,0:T(8,128)(2,1)} %param.20) | copy-start | bytes 2160004
  7.2 365.2 %all-reduce.7.cloned.1.call-start = ((), (), s32[]{:S(2)}) async-start(), calls=%async_computation.1 | async-start | bytes 8192000 | tf_op jit(solution)/shard_map/psum | solution.py:204
  21.4 16.4 %collective-permute-start = (bf16[300,3,3]{2,1,0:T(4,128)(2,1)}, bf16[300,3,3]{2,1,0:T(4,128)(2,1)S(1)}, u32[]{:S(2)}, u32[]{:S(2)}) collective-permute-start(bf16[300,3,3]{2,1,0:T(4,128)(2,1)} %get-tuple-element.179), channel_id=1, source_target_pairs={{0,4},{4,8},{8,12},{12,16},{16,20},{20,24},{24,28},{28,0},{1,5},{5... | collective-permute-start | bytes 16208 | tf_op jit(solution)/shard_map/ppermute | solution.py:17
  24.4 15.6 %collective-permute-start.1 = (bf16[300,3,3]{2,1,0:T(4,128)(2,1)}, bf16[300,3,3]{2,1,0:T(4,128)(2,1)}, u32[]{:S(2)}, u32[]{:S(2)}) collective-permute-start(bf16[300,3,3]{2,1,0:T(4,128)(2,1)} %get-tuple-element.180), channel_id=1, source_target_pairs={{4,0},{8,4},{12,8},{16,12},{20,16},{24,20},{28,24},{0,28},{5,1},{9... | collective-permute-start | bytes 16208 | tf_op jit(solution)/shard_map/ppermute | solution.py:18
  42.9 7.8 %collective-permute-start.3 = (bf16[300,3,134]{0,2,1:T(8,128)(2,1)}, bf16[300,3,134]{0,2,1:T(8,128)(2,1)}, u32[]{:S(2)}, u32[]{:S(2)}) collective-permute-start(bf16[300,3,134]{0,2,1:T(8,128)(2,1)} %copy.86), channel_id=1, source_target_pairs={{1,0},{2,1},{3,2},{0,3},{5,4},{6,5},{7,6},{4,7},{9,8},{10,9},{11,1... | collective-permute-start | bytes 723608 | tf_op jit(solution)/shard_map/ppermute | solution.py:18
  42.9 10.1 %collective-permute-start.2 = (bf16[300,3,134]{0,2,1:T(8,128)(2,1)}, bf16[300,3,134]{0,2,1:T(8,128)(2,1)}, u32[]{:S(2)}, u32[]{:S(2)}) collective-permute-start(bf16[300,3,134]{0,2,1:T(8,128)(2,1)} %copy.86), channel_id=1, source_target_pairs={{0,1},{1,2},{2,3},{3,0},{4,5},{5,6},{6,7},{7,4},{8,9},{9,10},{10,1... | collective-permute-start | bytes 723608 | tf_op jit(solution)/shard_map/ppermute | solution.py:17
  50.7 58.7 %copy-start.29 = (f32[300]{0:T(512)}, f32[300]{0:T(512)S(1)}, u32[]{:S(2)}) copy-start(f32[300]{0:T(512)S(1)} %get-tuple-element.117) | copy-start | bytes 3604
  50.7 58.7 %copy-start.31 = (f32[300]{0:T(512)}, f32[300]{0:T(512)S(1)}, u32[]{:S(2)}) copy-start(f32[300]{0:T(512)S(1)} %get-tuple-element.118) | copy-start | bytes 3604
  50.7 58.7 %copy-start.33 = (f32[300]{0:T(512)}, f32[300]{0:T(512)S(1)}, u32[]{:S(2)}) copy-start(f32[300]{0:T(512)S(1)} %get-tuple-element.119) | copy-start | bytes 3604
  59.6 15.3 %copy-start.14 = (bf16[4,75,384]{2,1,0:T(8,128)(2,1)S(1)}, bf16[4,75,384]{2,1,0:T(8,128)(2,1)}, u32[]{:S(2)}) copy-start(bf16[4,75,384]{2,1,0:T(8,128)(2,1)} %copy-done.13) | copy-start | bytes 691204
  62.9 21.7 %copy-start.8 = (f32[300,384]{1,0:T(8,128)S(1)}, f32[300,384]{1,0:T(8,128)}, u32[]{:S(2)}) copy-start(f32[300,384]{1,0:T(8,128)} %reshape.525) | copy-start | bytes 1382404
  62.9 21.7 %copy-start.9 = (f32[38,8,3,128]{3,1,2,0:T(8,128)S(1)}, f32[38,8,3,128]{3,1,2,0:T(8,128)}, u32[]{:S(2)}) copy-start(f32[38,8,3,128]{3,1,2,0:T(8,128)} %copy.111) | copy-start | bytes 1400836
  62.9 9.4 %collective-permute-start.4 = (bf16[300,3,134]{0,2,1:T(8,128)(2,1)}, bf16[300,3,134]{0,2,1:T(8,128)(2,1)S(1)}, u32[]{:S(2)}, u32[]{:S(2)}) collective-permute-start(bf16[300,3,134]{0,2,1:T(8,128)(2,1)} %copy.90), channel_id=1, source_target_pairs={{0,4},{4,0},{8,12},{12,8},{16,20},{20,16},{24,28},{28,24},{1,5},{5... | collective-permute-start | bytes 723608 | tf_op jit(solution)/shard_map/ppermute | solution.py:24
  72.2 10.3 %collective-permute-start.5 = (bf16[300,3,134]{0,2,1:T(8,128)(2,1)S(1)}, bf16[300,3,134]{0,2,1:T(8,128)(2,1)S(1)}, u32[]{:S(2)}, u32[]{:S(2)}) collective-permute-start(bf16[300,3,134]{0,2,1:T(8,128)(2,1)S(1)} %collective-permute-done.4), channel_id=1, source_target_pairs={{0,8},{4,12},{8,0},{12,4},{16,24},{20,28},{24,16},{28,20},{1,9},{5... | collective-permute-start | bytes 723608 | tf_op jit(solution)/shard_map/ppermute | solution.py:24
  82.5 15.9 %collective-permute-start.6 = (bf16[300,3,134]{0,2,1:T(8,128)(2,1)S(1)}, bf16[300,3,134]{0,2,1:T(8,128)(2,1)}, u32[]{:S(2)}, u32[]{:S(2)}) collective-permute-start(bf16[300,3,134]{0,2,1:T(8,128)(2,1)S(1)} %collective-permute-done.5), channel_id=1, source_target_pairs={{0,16},{4,20},{8,24},{12,28},{16,0},{20,4},{24,8},{28,12},{1,17},{... | collective-permute-start | bytes 723608 | tf_op jit(solution)/shard_map/ppermute | solution.py:24
  109.4 37.2 %copy-start.2 = (f32[300,9,134]{2,1,0:T(8,128)}, f32[300,9,134]{2,1,0:T(8,128)S(1)}, u32[]{:S(2)}) copy-start(f32[300,9,134]{2,1,0:T(8,128)S(1)} %maximum_convert_fusion) | copy-start | bytes 4341604
  220.4 36.1 %copy-start.75 = (f32[384]{0:T(512)S(1)}, f32[384]{0:T(512)}, u32[]{:S(2)}) copy-start(f32[384]{0:T(512)} %copy-done.74) | copy-start | bytes 4612
  220.4 36.1 %copy-start.77 = (f32[384]{0:T(512)S(1)}, f32[384]{0:T(512)}, u32[]{:S(2)}) copy-start(f32[384]{0:T(512)} %copy-done.76) | copy-start | bytes 4612
  260.6 14.0 %collective-permute-start.7 = (bf16[300,3,3]{2,1,0:T(4,128)(2,1)S(1)}, bf16[300,3,3]{2,1,0:T(4,128)(2,1)S(1)}, u32[]{:S(2)}, u32[]{:S(2)}) collective-permute-start(bf16[300,3,3]{2,1,0:T(4,128)(2,1)S(1)} %get-tuple-element.177), channel_id=1, source_target_pairs={{0,4},{4,8},{8,12},{12,16},{16,20},{20,24},{24,28},{28,0},{1,5},{5... | collective-permute-start | bytes 16208 | tf_op jit(solution)/shard_map/ppermute | solution.py:17
  262.2 14.6 %collective-permute-start.8 = (bf16[300,3,3]{2,1,0:T(4,128)(2,1)S(1)}, bf16[300,3,3]{2,1,0:T(4,128)(2,1)S(1)}, u32[]{:S(2)}, u32[]{:S(2)}) collective-permute-start(bf16[300,3,3]{2,1,0:T(4,128)(2,1)S(1)} %get-tuple-element.178), channel_id=1, source_target_pairs={{4,0},{8,4},{12,8},{16,12},{20,16},{24,20},{28,24},{0,28},{5,1},{9... | collective-permute-start | bytes 16208 | tf_op jit(solution)/shard_map/ppermute | solution.py:18
  265.6 261.2 %all-reduce.5.cloned.1.call-start = ((), (), s32[]{:S(2)}) async-start(), calls=%async_computation | async-start | bytes 8192000 | tf_op jit(solution)/shard_map/psum | solution.py:203
  278.0 15.3 %collective-permute-start.10 = (bf16[300,3,134]{0,2,1:T(8,128)(2,1)S(1)}, bf16[300,3,134]{0,2,1:T(8,128)(2,1)}, u32[]{:S(2)}, u32[]{:S(2)}) collective-permute-start(bf16[300,3,134]{0,2,1:T(8,128)(2,1)S(1)} %copy.97), channel_id=1, source_target_pairs={{1,0},{2,1},{3,2},{0,3},{5,4},{6,5},{7,6},{4,7},{9,8},{10,9},{11,1... | collective-permute-start | bytes 723608 | tf_op jit(solution)/shard_map/ppermute | solution.py:18
  278.9 16.4 %collective-permute-start.9 = (bf16[300,3,134]{0,2,1:T(8,128)(2,1)S(1)}, bf16[300,3,134]{0,2,1:T(8,128)(2,1)S(1)}, u32[]{:S(2)}, u32[]{:S(2)}) collective-permute-start(bf16[300,3,134]{0,2,1:T(8,128)(2,1)S(1)} %copy.97), channel_id=1, source_target_pairs={{0,1},{1,2},{2,3},{3,0},{4,5},{5,6},{6,7},{7,4},{8,9},{9,10},{10,1... | collective-permute-start | bytes 723608 | tf_op jit(solution)/shard_map/ppermute | solution.py:17
  301.2 16.2 %copy-start.10 = (f32[38,8,3,128]{3,1,2,0:T(8,128)S(1)}, f32[38,8,3,128]{3,1,2,0:T(8,128)}, u32[]{:S(2)}) copy-start(f32[38,8,3,128]{3,1,2,0:T(8,128)} %copy.109) | copy-start | bytes 1400836
  301.2 16.2 %copy-start.22 = (bf16[1200,300]{0,1:T(8,128)(2,1)S(1)}, bf16[1200,300]{0,1:T(8,128)(2,1)}, u32[]{:S(2)}) copy-start(bf16[1200,300]{0,1:T(8,128)(2,1)} %param.21) | copy-start | bytes 2160004
  301.2 16.2 %copy-start.73 = (f32[384]{0:T(512)S(1)}, f32[384]{0:T(512)}, u32[]{:S(2)}) copy-start(f32[384]{0:T(512)} %copy-done.72) | copy-start | bytes 4612
  301.9 14.4 %collective-permute-start.11 = (bf16[300,3,134]{0,2,1:T(8,128)(2,1)S(1)}, bf16[300,3,134]{0,2,1:T(8,128)(2,1)}, u32[]{:S(2)}, u32[]{:S(2)}) collective-permute-start(bf16[300,3,134]{0,2,1:T(8,128)(2,1)S(1)} %copy.101), channel_id=1, source_target_pairs={{0,4},{4,0},{8,12},{12,8},{16,20},{20,16},{24,28},{28,24},{1,5},{5... | collective-permute-start | bytes 723608 | tf_op jit(solution)/shard_map/ppermute | solution.py:24
  316.3 9.7 %collective-permute-start.12 = (bf16[300,3,134]{0,2,1:T(8,128)(2,1)}, bf16[300,3,134]{0,2,1:T(8,128)(2,1)S(1)}, u32[]{:S(2)}, u32[]{:S(2)}) collective-permute-start(bf16[300,3,134]{0,2,1:T(8,128)(2,1)} %collective-permute-done.11), channel_id=1, source_target_pairs={{0,8},{4,12},{8,0},{12,4},{16,24},{20,28},{24,16},{28,20},{1,9},{5... | collective-permute-start | bytes 723608 | tf_op jit(solution)/shard_map/ppermute | solution.py:24
  326.0 42.3 %collective-permute-start.13 = (bf16[300,3,134]{0,2,1:T(8,128)(2,1)S(1)}, bf16[300,3,134]{0,2,1:T(8,128)(2,1)S(1)}, u32[]{:S(2)}, u32[]{:S(2)}) collective-permute-start(bf16[300,3,134]{0,2,1:T(8,128)(2,1)S(1)} %collective-permute-done.12), channel_id=1, source_target_pairs={{0,16},{4,20},{8,24},{12,28},{16,0},{20,4},{24,8},{28,12},{1,17},{... | collective-permute-start | bytes 723608 | tf_op jit(solution)/shard_map/ppermute | solution.py:24
  387.3 14.4 %copy-start.17 = (bf16[300,3,128]{2,0,1:T(8,128)(2,1)S(1)}, bf16[300,3,128]{2,0,1:T(8,128)(2,1)}, u32[]{:S(2)}) copy-start(bf16[300,3,128]{2,0,1:T(8,128)(2,1)} %param.17) | copy-start | bytes 691204
  387.3 14.4 %copy-start.79 = (f32[300]{0:T(512)S(1)}, f32[300]{0:T(512)}, u32[]{:S(2)}) copy-start(f32[300]{0:T(512)} %get-tuple-element.154) | copy-start | bytes 3604
  387.3 14.4 %copy-start.81 = (f32[300]{0:T(512)S(1)}, f32[300]{0:T(512)}, u32[]{:S(2)}) copy-start(f32[300]{0:T(512)} %get-tuple-element.155) | copy-start | bytes 3604
  387.3 14.4 %copy-start.83 = (f32[300]{0:T(512)S(1)}, f32[300]{0:T(512)}, u32[]{:S(2)}) copy-start(f32[300]{0:T(512)} %get-tuple-element.156) | copy-start | bytes 3604
  387.3 14.4 %copy-start.85 = (f32[300]{0:T(512)S(1)}, f32[300]{0:T(512)}, u32[]{:S(2)}) copy-start(f32[300]{0:T(512)} %get-tuple-element.157) | copy-start | bytes 3604
  387.3 14.4 %copy-start.87 = (f32[300]{0:T(512)S(1)}, f32[300]{0:T(512)}, u32[]{:S(2)}) copy-start(f32[300]{0:T(512)} %get-tuple-element.158) | copy-start | bytes 3604
  387.3 14.4 %copy-start.89 = (f32[300]{0:T(512)S(1)}, f32[300]{0:T(512)}, u32[]{:S(2)}) copy-start(f32[300]{0:T(512)} %get-tuple-element.159) | copy-start | bytes 3604
  387.3 14.4 %copy-start.91 = (f32[300]{0:T(512)S(1)}, f32[300]{0:T(512)}, u32[]{:S(2)}) copy-start(f32[300]{0:T(512)} %get-tuple-element.160) | copy-start | bytes 3604
  387.3 14.4 %copy-start.93 = (f32[300]{0:T(512)S(1)}, f32[300]{0:T(512)}, u32[]{:S(2)}) copy-start(f32[300]{0:T(512)} %get-tuple-element.161) | copy-start | bytes 3604
  387.3 14.4 %copy-start.95 = (f32[300]{0:T(512)S(1)}, f32[300]{0:T(512)}, u32[]{:S(2)}) copy-start(f32[300]{0:T(512)} %get-tuple-element.162) | copy-start | bytes 3604
  387.4 14.4 %copy-start.97 = (f32[300]{0:T(512)S(1)}, f32[300]{0:T(512)}, u32[]{:S(2)}) copy-start(f32[300]{0:T(512)} %get-tuple-element.163) | copy-start | bytes 3604
  387.4 14.4 %copy-start.99 = (f32[300]{0:T(512)S(1)}, f32[300]{0:T(512)}, u32[]{:S(2)}) copy-start(f32[300]{0:T(512)} %get-tuple-element.164) | copy-start | bytes 3604
  387.4 14.4 %copy-start.101 = (f32[300]{0:T(512)S(1)}, f32[300]{0:T(512)}, u32[]{:S(2)}) copy-start(f32[300]{0:T(512)} %get-tuple-element.135) | copy-start | bytes 3604
  387.4 14.4 %copy-start.103 = (f32[300]{0:T(512)S(1)}, f32[300]{0:T(512)}, u32[]{:S(2)}) copy-start(f32[300]{0:T(512)} %get-tuple-element.139) | copy-start | bytes 3604
  387.4 14.4 %copy-start.105 = (f32[300]{0:T(512)S(1)}, f32[300]{0:T(512)}, u32[]{:S(2)}) copy-start(f32[300]{0:T(512)} %get-tuple-element.140) | copy-start | bytes 3604
  387.4 14.4 %copy-start.107 = (f32[300]{0:T(512)S(1)}, f32[300]{0:T(512)}, u32[]{:S(2)}) copy-start(f32[300]{0:T(512)} %get-tuple-element.141) | copy-start | bytes 3604
  387.4 14.4 %copy-start.109 = (f32[300]{0:T(512)S(1)}, f32[300]{0:T(512)}, u32[]{:S(2)}) copy-start(f32[300]{0:T(512)} %get-tuple-element.142) | copy-start | bytes 3604
  387.4 14.4 %copy-start.111 = (f32[300]{0:T(512)S(1)}, f32[300]{0:T(512)}, u32[]{:S(2)}) copy-start(f32[300]{0:T(512)} %get-tuple-element.143) | copy-start | bytes 3604
  387.4 14.4 %copy-start.113 = (f32[300]{0:T(512)S(1)}, f32[300]{0:T(512)}, u32[]{:S(2)}) copy-start(f32[300]{0:T(512)} %get-tuple-element.144) | copy-start | bytes 3604
  (97 other events, 451.4 us)
Sparse Core Ops, SparseCore 0:
  265.7 90.8 all-reduce.6
  372.7 154.0 all-reduce.4
